TPU v7x, 32 devices: a whole 2x2x4 slice. The times are simulated.
32 devices in a mesh: dp: 8 (over z, x), mp: 4 (over y, core).
Axes of the slice: x: 2, y: 2, z: 4, core: 2. Of those that a mesh axis runs over, the one named last changes fastest.
Arguments:
- tokens: bfloat16 [16384, 512], P('dp'), may hold values from -6 to 6
- cotangent: bfloat16 [16384, 512], P('dp'), may hold values from -6 to 6
- bucket: int32 [16384, 1], P('dp'), may hold values from 0 to 7, as said below
- cell: int32 [16384], P('dp'), may hold values from 0 to 1, as said below
- features: bfloat16 [4, 64, 256], replicated, may hold values from -4 to 4
- qkv_weight: bfloat16 [3, 512, 512], P(None, None, 'mp'), may hold values from -0.25 to 0.25
- out_weight: bfloat16 [512, 512], P('mp'), may hold values from -1 to 1
- out_bias: float32 [512], replicated, may hold values from -3 to 3
- norm1_gain: float32 [512], replicated, may hold values from 0.25 to 1.75
- norm1_bias: float32 [512], replicated, may hold values from -3 to 3
- norm2_gain: float32 [512], replicated, may hold values from 0.25 to 1.75
- norm2_bias: float32 [512], replicated, may hold values from -3 to 3
- up_weight: bfloat16 [512, 2048], P(None, 'mp'), may hold values from -0.25 to 0.25
- up_bias: float32 [2048], P('mp'), may hold values from -3 to 3
- down_weight: bfloat16 [2048, 512], P('mp'), may hold values from -0.125 to 0.125
- down_bias: float32 [512], replicated, may hold values from -3 to 3
Outputs:
- output: bfloat16 [16384, 512], P('dp')
- grad_tokens: float32 [16384, 512], P('dp')
- grad_qkv_weight: float32 [3, 512, 512], P(None, None, 'mp')
- grad_out_weight: float32 [512, 512], P('mp')
- grad_out_bias: float32 [512], replicated
- grad_norm1_gain: float32 [512], replicated
- grad_norm1_bias: float32 [512], replicated
- grad_norm2_gain: float32 [512], replicated
- grad_norm2_bias: float32 [512], replicated
- grad_up_weight: float32 [512, 2048], P(None, 'mp')
- grad_up_bias: float32 [2048], P('mp')
- grad_down_weight: float32 [2048, 512], P('mp')
- grad_down_bias: float32 [512], replicated
Inputs may be any that keep to these rules, and one draw needn't show every extreme that they name: The 2048 rows of one device name every bucket at least once and one bucket at most 512 times, and every device names some bucket exactly 512 times. In every bucket one cell, drawn from the seed, holds tokens from every device.
All inputs are finite; a program needn't handle non-finite values.
Results may differ from a plain program's by a relative error of at most 0.012.
The roundings to bfloat16 on the way count: a program that leaves them out, or rounds other values in their place, can miss the bound.
Values may be sent and summed in bfloat16 or wider, within the bound.
A program may use at most 192 MiB of HBM per device.

v0:
```python
import jax
import jax.numpy as jnp
from jax import lax
from jax.sharding import PartitionSpec as P

HD = 64
FEATS = 4
STEP = 5
SEG = 2
EXACT_PRECISION = lax.Precision.HIGHEST


def layer_norm(values, norm_gain, norm_bias):
    average = jnp.mean(values, -1, keepdims=True)
    centred = values - average
    spread = jnp.mean(centred * centred, -1, keepdims=True)
    return centred * lax.rsqrt(spread + 1e-05) * norm_gain + norm_bias


def exact_gelu(values):
    return jax.nn.gelu(values, approximate=False)


def rounded(values):
    return lax.optimization_barrier(values.astype(jnp.bfloat16)).astype(jnp.float32)


def feature_map(rows, feature_rows):
    scale = HD ** (-0.25)
    projected = (
        jnp.einsum("thd,dm->thm", rows, feature_rows, preferred_element_type=jnp.float32) * scale
    )
    widened = rows.astype(jnp.float32)
    squares = 0.5 * scale * scale * jnp.sum(widened * widened, -1, keepdims=True)
    return jnp.exp(projected - squares)


def feature_back(rows, feature_rows, feats, grad_feats):
    scale = HD ** (-0.25)
    weighted = grad_feats * feats
    widened = rows.astype(jnp.float32)
    spread_back = jnp.einsum(
        "thm,dm->thd", weighted, feature_rows.astype(jnp.float32), precision=EXACT_PRECISION
    )
    return scale * spread_back - scale * scale * widened * jnp.sum(weighted, -1, keepdims=True)


def per_device(
    tokens,
    cotangent,
    bucket,
    cell,
    features,
    qkv_weight,
    out_weight,
    out_bias,
    norm1_gain,
    norm1_bias,
    norm2_gain,
    norm2_bias,
    up_weight,
    up_bias,
    down_weight,
    down_bias,
):
    bucket_count = lax.axis_size("dp")
    token_count = tokens.shape[0]
    local_width = qkv_weight.shape[2]
    heads_local = local_width // HD
    capacity = 2 * token_count // bucket_count
    slots = bucket_count * capacity
    target = bucket[:, 0]
    membership = (target[:, None] == jnp.arange(bucket_count, dtype=jnp.int32)[None, :]).astype(
        jnp.int32
    )
    rank_within = jnp.sum(jnp.cumsum(membership, 0) * membership, 1) - 1
    slot_index = target * capacity + rank_within

    def to_slots(rows):
        return jnp.zeros((slots,) + rows.shape[1:], rows.dtype).at[slot_index].set(rows)

    def home_rows(partial_rows):
        returned = lax.all_to_all(partial_rows, "dp", split_axis=0, concat_axis=0, tiled=True)
        return lax.psum(returned[slot_index], "mp").astype(jnp.bfloat16)

    def over_units(partial_rows):
        return lax.psum(partial_rows, "mp")

    residual = tokens.astype(jnp.float32)
    normed, norm1_back = jax.vjp(layer_norm, residual, norm1_gain, norm1_bias)
    normed_low = normed.astype(jnp.bfloat16)
    cell_labels = (cell + 1).astype(jnp.bfloat16)
    received, slot_cells = (
        lax.all_to_all(to_slots(normed_low), "dp", split_axis=0, concat_axis=0, tiled=True),
        lax.all_to_all(to_slots(cell_labels), "dp", split_axis=0, concat_axis=0, tiled=True),
    )
    projected = jnp.einsum(
        "td,cde->tce", received, qkv_weight, preferred_element_type=jnp.float32
    ).astype(jnp.bfloat16)
    labels_wide = slot_cells.astype(jnp.float32)
    cell_masks = (
        labels_wide[:, None] == jnp.arange(1, SEG + 1, dtype=jnp.float32)[None, :]
    ).astype(jnp.float32)
    occupied = jnp.sum(cell_masks, 1)
    masks_low = cell_masks.astype(jnp.bfloat16)
    query = projected[:, 0].reshape(slots, heads_local, HD)
    key_rows = projected[:, 1].reshape(slots, heads_local, HD)
    value_matrix_rows = projected[:, 2].reshape(slots, heads_local, HD)
    feature_rows = features[STEP % FEATS]
    query_wide = feature_map(query, feature_rows)
    key_wide = feature_map(key_rows, feature_rows)
    query_feature_map = query_wide.astype(jnp.bfloat16)
    key_feature_map = key_wide.astype(jnp.bfloat16)
    attention_numerator = jnp.zeros((slots, heads_local, HD), jnp.float32)
    denominator = jnp.broadcast_to((1.0 - occupied)[:, None], (slots, heads_local))
    cell_states = []
    cell_totals = []
    for part_index in range(SEG):
        weight_col = cell_masks[:, part_index]
        cell_memory_state = jnp.einsum(
            "ciu,cib->iub",
            key_feature_map * masks_low[:, part_index, None, None],
            value_matrix_rows,
            preferred_element_type=jnp.float32,
        ).astype(jnp.bfloat16)
        cell_total = jnp.einsum(
            "thm,t->hm",
            key_feature_map,
            masks_low[:, part_index],
            preferred_element_type=jnp.float32,
        )
        attention_numerator = attention_numerator + weight_col[:, None, None] * jnp.einsum(
            "fba,bay->fby", query_feature_map, cell_memory_state, preferred_element_type=jnp.float32
        )
        denominator = denominator + weight_col[:, None] * jnp.einsum(
            "thm,hm->th",
            query_feature_map,
            cell_total,
            precision=EXACT_PRECISION,
            preferred_element_type=jnp.float32,
        )
        cell_states.append(cell_memory_state)
        cell_totals.append(cell_total)
    attention = (
        (attention_numerator / denominator[..., None])
        .reshape(slots, local_width)
        .astype(jnp.bfloat16)
    )
    branch = home_rows(jnp.dot(attention, out_weight, preferred_element_type=jnp.float32))
    midstream = residual + branch.astype(jnp.float32) + out_bias
    normed2, norm2_back = jax.vjp(layer_norm, midstream, norm2_gain, norm2_bias)
    normed2_low = normed2.astype(jnp.bfloat16)
    preact = jnp.dot(normed2_low, up_weight, preferred_element_type=jnp.float32) + up_bias
    active, gelu_back = jax.vjp(exact_gelu, preact)
    active_low = active.astype(jnp.bfloat16)
    branch_out = over_units(jnp.dot(active_low, down_weight, preferred_element_type=jnp.float32))
    output = (midstream + branch_out + down_bias).astype(jnp.bfloat16)
    upstream = cotangent.astype(jnp.float32)
    contract_rows = (((0,), (0,)), ((), ()))
    grad_down_bias = jnp.sum(upstream, 0)
    grad_down_weight = lax.dot_general(
        active_low, cotangent, contract_rows, preferred_element_type=jnp.float32
    )
    (grad_preact,) = gelu_back(
        jnp.dot(cotangent, down_weight.T, preferred_element_type=jnp.float32)
    )
    grad_preact_low = grad_preact.astype(jnp.bfloat16)
    grad_up_bias = jnp.sum(grad_preact_low.astype(jnp.float32), 0)
    grad_up_weight = lax.dot_general(
        normed2_low, grad_preact_low, contract_rows, preferred_element_type=jnp.float32
    )
    grad_normed2 = over_units(
        jnp.dot(grad_preact_low, up_weight.T, preferred_element_type=jnp.float32)
    )
    grad_mid_norm, grad_norm2_gain, grad_norm2_bias = norm2_back(grad_normed2)
    grad_midstream = upstream + grad_mid_norm
    grad_out_bias = jnp.sum(grad_midstream, 0)
    grad_branch = grad_midstream.astype(jnp.bfloat16)
    arrived = lax.all_to_all(to_slots(grad_branch), "dp", split_axis=0, concat_axis=0, tiled=True)
    grad_out_weight = lax.dot_general(
        attention, arrived, contract_rows, preferred_element_type=jnp.float32
    )
    grad_attention = rounded(jnp.dot(arrived, out_weight.T, preferred_element_type=jnp.float32))
    grad_attention = grad_attention.reshape(slots, heads_local, HD)
    grad_numerator = grad_attention / denominator[..., None]
    grad_denominator = -jnp.sum(grad_attention * attention_numerator, -1) / (
        denominator * denominator
    )
    grad_query_feat = jnp.zeros((slots, heads_local, query_feature_map.shape[2]), jnp.float32)
    grad_key_feat = jnp.zeros_like(grad_query_feat)
    grad_value = jnp.zeros((slots, heads_local, HD), jnp.float32)
    for part_index in range(SEG):
        weight_col = cell_masks[:, part_index]
        numer_masked = grad_numerator * weight_col[:, None, None]
        denom_masked = grad_denominator * weight_col[:, None]
        grad_state = jnp.einsum(
            "ciu,cib->iub",
            query_feature_map,
            numer_masked,
            precision=EXACT_PRECISION,
            preferred_element_type=jnp.float32,
        )
        grad_total = jnp.einsum(
            "thm,th->hm",
            query_feature_map,
            denom_masked,
            precision=EXACT_PRECISION,
            preferred_element_type=jnp.float32,
        )
        grad_query_feat = (
            grad_query_feat
            + jnp.einsum(
                "peo,exo->pex",
                numer_masked,
                cell_states[part_index],
                precision=EXACT_PRECISION,
                preferred_element_type=jnp.float32,
            )
            + denom_masked[..., None] * cell_totals[part_index][None]
        )
        grad_key_feat = grad_key_feat + weight_col[:, None, None] * (
            jnp.einsum(
                "peo,exo->pex",
                value_matrix_rows,
                grad_state,
                precision=EXACT_PRECISION,
                preferred_element_type=jnp.float32,
            )
            + grad_total[None]
        )
        grad_value = grad_value + weight_col[:, None, None] * jnp.einsum(
            "fba,bay->fby",
            key_feature_map,
            grad_state,
            precision=EXACT_PRECISION,
            preferred_element_type=jnp.float32,
        )
    grad_query = feature_back(query, feature_rows, query_wide, grad_query_feat)
    grad_key = feature_back(key_rows, feature_rows, key_wide, grad_key_feat)
    grad_projected = jnp.stack(
        [
            grad_query.reshape(slots, local_width),
            grad_key.reshape(slots, local_width),
            grad_value.reshape(slots, local_width),
        ],
        1,
    ).astype(jnp.bfloat16)
    grad_qkv_weight = jnp.einsum(
        "td,tce->cde", received, grad_projected, preferred_element_type=jnp.float32
    )
    grad_normed = home_rows(
        jnp.einsum("tce,cde->td", grad_projected, qkv_weight, preferred_element_type=jnp.float32)
    )
    grad_residual, grad_norm1_gain, grad_norm1_bias = norm1_back(grad_normed.astype(jnp.float32))
    grad_tokens = grad_midstream + grad_residual
    summed = lax.psum(
        (
            grad_qkv_weight,
            grad_out_weight,
            grad_out_bias,
            grad_norm1_gain,
            grad_norm1_bias,
            grad_norm2_gain,
            grad_norm2_bias,
            grad_up_weight,
            grad_up_bias,
            grad_down_weight,
            grad_down_bias,
        ),
        "dp",
    )
    return (
        output,
        grad_tokens,
        summed[0],
        summed[1],
        summed[2],
        summed[3],
        summed[4],
        summed[5],
        summed[6],
        summed[7],
        summed[8],
        summed[9],
        summed[10],
    )


def solution(mesh):
    return jax.shard_map(
        per_device,
        mesh=mesh,
        in_specs=(
            P("dp", None),
            P("dp", None),
            P("dp", None),
            P("dp"),
            P(),
            P(None, None, "mp"),
            P("mp", None),
            P(),
            P(),
            P(),
            P(),
            P(),
            P(None, "mp"),
            P("mp"),
            P("mp", None),
            P(),
        ),
        out_specs=(
            P("dp", None),
            P("dp", None),
            P(None, None, "mp"),
            P("mp", None),
            P(),
            P(),
            P(),
            P(),
            P(),
            P(None, "mp"),
            P("mp"),
            P("mp", None),
            P(),
        ),
        check_vma=False,
    )
```

profile of v0, /device:TPU:0, one launch (start us, length us, event | category | flops | bytes accessed | tf_op | source)
XLA Modules:
  0.0 1306.6 jit_solution(10532565975702089205)
XLA Ops:
  13.1 14.6 %scatter_custom_fusion = bf16[4096]{0:T(1024)(128)(2,1)S(1)} fusion(s32[2048]{0:T(1024)S(1)} %bitcast.227, bf16[2048]{0:T(1024)(128)(2,1)S(1)} %add_convert_fusion.3, bf16[]{:T(256)} %constant.43.clone.1), kind=kCustom, calls=%fused_computation.181 | custom fusion | bytes 8194 | tf_op jit(solution)/shard_map/scatter | solution.py:80
  29.5 7.3 all-to-all-start
  40.4 13.3 %scatter_custom_fusion.1 = bf16[4096,512]{1,0:T(8,128)(2,1)} fusion(s32[2048]{0:T(1024)S(1)} %bitcast.228, bf16[2048,512]{1,0:T(8,128)(2,1)S(1)} %copy-done.7, f32[512]{0:T(512)S(1)} %copy-done.52, f32[512]{0:T(512)S(1)} %copy-done.48, f32[2048]{0:T(1024)S(1)} %fusion.100, f32[2048]{0:T(1024)S(1)} %broadcast_multiply_fusion.7, bf16[]{:T(256)} %constant.43.clone.1), kind=kCustom, calls=%fused_computation.89 | custom fusion | flops 6291456 | bytes 6311938 | tf_op jit(solution)/shard_map/scatter | solution.py:80
  53.7 6.4 all-to-all-start.1
  60.7 91.9 %all-to-all-done.1 = bf16[8,512,512]{2,1,0:T(8,128)(2,1)} async-done(((bf16[8,512,512]{2,1,0:T(8,128)(2,1)}), bf16[8,512,512]{2,1,0:T(8,128)(2,1)}, u32[]{:S(2)}, u32[]{:S(2)}) %all-to-all-start.1) | async-done | bytes 4194336 | tf_op jit(solution)/shard_map/all_to_all | solution.py:94
  152.6 4.0 fusion.120
  157.9 5.1 fusion.2
  168.5 5.1 fusion.3
  175.4 11.8 fusion.106
  188.2 2.4 divide_convert_fusion
  191.9 4.6 fusion.65
  196.6 5.0 all-to-all-start.2
  201.6 181.9 %all-to-all-done.2 = f32[8,512,512]{2,1,0:T(8,128)} async-done(((f32[8,512,512]{2,1,0:T(8,128)}), f32[8,512,512]{2,1,0:T(8,128)}, u32[]{:S(2)}, u32[]{:S(2)}) %all-to-all-start.2) | async-done | bytes 8388640 | tf_op jit(solution)/shard_map/all_to_all | solution.py:83
  383.6 12.9 gather_fusion
  396.4 76.3 %all-reduce.11 = bf16[2048,512]{1,0:T(8,128)(2,1)} all-reduce(f32[2048,512]{1,0:T(8,128)} %gather_fusion), channel_id=1, replica_groups=mesh['dp'=8,'mp'=4] {'mp'}, use_global_device_ids=true, to_apply=%region_10.11 | all-reduce | flops 1048576 | bytes 6291456 | tf_op jit(solution)/shard_map/psum | solution.py:84
  472.7 2.5 fusion.35
  479.5 10.6 convert_reduce_fusion.3
  491.5 3.2 fusion.122
  494.7 3.2 fusion.121
  498.0 153.0 %all-reduce.10.cloned.1.call-done = (f32[2048,512]{1,0:T(8,128)}, f32[2048,512]{1,0:T(8,128)}) async-done(((f32[2048,512]{1,0:T(8,128)}, f32[2048,512]{1,0:T(8,128)}), (f32[2048,512]{1,0:T(8,128)}, f32[2048,512]{1,0:T(8,128)})) %all-reduce.10.cloned.1.call-update) | async-done | bytes 8388624 | tf_op jit(solution)/shard_map/psum | solution.py:87
  651.0 4.6 multiply_reduce_fusion
  656.9 2.7 fusion.114
  659.7 13.7 %scatter_custom_fusion.2 = bf16[4096,512]{1,0:T(8,128)(2,1)} fusion(s32[2048]{0:T(1024)S(1)} %bitcast.230, bf16[]{:T(256)} %constant.43.clone.1, bf16[2048,512]{1,0:T(8,128)(2,1)S(1)} %copy-done.27, f32[2048,512]{1,0:T(8,128)} %get-tuple-element.82, f32[2048]{0:T(1024)S(1)} %negate_multiply_fusion.2), kind=kCustom, calls=%fused_computation.91 | custom fusion | flops 4194304 | bytes 10493954 | tf_op jit(solution)/shard_map/scatter | solution.py:80
  673.3 98.9 %all_to_all.55 = bf16[8,512,512]{2,1,0:T(8,128)(2,1)S(1)} all-to-all(bf16[8,512,512]{2,1,0:T(8,128)(2,1)} %bitcast.189), channel_id=1, replica_groups=mesh['dp'=8,'mp'=4] {'dp'}, dimensions={0} | all-to-all | bytes 8388608 | tf_op jit(solution)/shard_map/all_to_all | solution.py:179
  780.7 3.9 fusion.51
  784.6 3.9 fusion.54
  788.6 2.3 convolution_multiply_fusion.1
  790.9 5.7 fusion.123
  796.6 5.9 fusion.56
  802.5 3.3 fusion.86
  805.9 3.4 fusion.84
  809.2 3.3 fusion.16
  814.8 10.6 fusion.118
  825.4 4.7 fusion.15
  832.4 10.4 fusion.119
  842.9 3.7 fusion.14
  848.2 7.2 fusion.58
  855.4 5.0 all-to-all-start.4
  860.5 4.6 fusion.125
  865.1 2.4 fusion.110
  869.4 4.9 convolution_bitcast_fusion
  874.4 276.7 %all-reduce.8.cloned.1.call-done = (f32[3,512,128]{1,2,0:T(8,128)}, f32[128,512]{1,0:T(8,128)}, f32[512,512]{1,0:T(8,128)}, f32[512,512]{1,0:T(8,128)}) async-done(((f32[3,512,128]{1,2,0:T(8,128)}, f32[128,512]{1,0:T(8,128)}, f32[512,512]{1,0:T(8,128)}, f32[512,512]{1,0:T(8,128)}), (f32[3,512,128]{1,2,0:T(8,128)}, f32[128,512]{1,0:T(8,128)}, f32[512,512]{1,0:T(8,128)}, ...) | async-done | bytes 3145744 | tf_op jit(solution)/shard_map/psum | solution.py:256
  1153.3 12.9 gather_fusion.1
  1166.2 77.7 %all-reduce.12 = bf16[2048,512]{1,0:T(8,128)(2,1)} all-reduce(f32[2048,512]{1,0:T(8,128)} %gather_fusion.1), channel_id=1, replica_groups=mesh['dp'=8,'mp'=4] {'mp'}, use_global_device_ids=true, to_apply=%region_21.22 | all-reduce | flops 1048576 | bytes 6291456 | tf_op jit(solution)/shard_map/psum | solution.py:84
  1244.0 3.4 convert_reduce_fusion
  1247.5 3.6 fusion.24
  1251.1 7.5 convert_reduce_fusion.2
  1258.6 35.4 %all-reduce = (f32[512]{0:T(512)}, f32[512]{0:T(512)}, f32[512]{0:T(512)}, f32[512]{0:T(512)}, f32[512]{0:T(512)}, /*index=5*/f32[512]{0:T(512)}, f32[512]{0:T(512)}) all-reduce(f32[512]{0:T(512)S(1)} %get-tuple-element.58, f32[512]{0:T(512)S(1)} %get-tuple-element.54, ...), channel_id=1, replica_groups=mesh['dp'=8,'mp'=4] {'dp'}, use_global_device_ids=true, to_apply=%region_27.28 | all-reduce | flops 3584 | bytes 28672 | tf_op jit(solution)/shard_map/psum | solution.py:256
  (185 shorter events, 53.7 us)
Async XLA Ops:
  7.2 471.3 %copy-start = (bf16[512,512]{1,0:T(8,128)(2,1)S(1)}, bf16[512,512]{1,0:T(8,128)(2,1)}, u32[]{:S(2)}) copy-start(bf16[512,512]{1,0:T(8,128)(2,1)} %param.30) | copy-start | bytes 1572868
  7.2 31.5 %copy-start.7 = (bf16[2048,512]{1,0:T(8,128)(2,1)S(1)}, bf16[2048,512]{1,0:T(8,128)(2,1)}, u32[]{:S(2)}) copy-start(bf16[2048,512]{1,0:T(8,128)(2,1)} %param.16) | copy-start | bytes 6291460
  7.2 33.2 %copy-start.48 = (f32[512]{0:T(512)S(1)}, f32[512]{0:T(512)}, u32[]{:S(2)}) copy-start(f32[512]{0:T(512)} %param.24) | copy-start | bytes 6148
  7.2 33.1 %copy-start.52 = (f32[512]{0:T(512)S(1)}, f32[512]{0:T(512)}, u32[]{:S(2)}) copy-start(f32[512]{0:T(512)} %param.25) | copy-start | bytes 6148
  29.5 24.2 %all-to-all-start = ((bf16[8,2,256]{2,1,0:T(2,128)(2,1)}), bf16[8,2,256]{2,1,0:T(2,128)(2,1)S(1)}, u32[]{:S(2)}, u32[]{:S(2)}) async-start(bf16[8,2,256]{2,1,0:T(2,128)(2,1)} %reshape.249), calls=%async_computation | async-start | bytes 16384 | tf_op jit(solution)/shard_map/all_to_all | solution.py:95
  38.7 14.9 %copy-start.38 = (f32[2048]{0:T(1024)}, f32[2048]{0:T(1024)S(1)}, u32[]{:S(2)}) copy-start(f32[2048]{0:T(1024)S(1)} %broadcast_multiply_fusion.7) | copy-start | bytes 24580
  40.4 13.3 %copy-start.42 = (f32[2048]{0:T(1024)}, f32[2048]{0:T(1024)S(1)}, u32[]{:S(2)}) copy-start(f32[2048]{0:T(1024)S(1)} %fusion.100) | copy-start | bytes 24580
  53.7 6.4 copy-start.36
  53.7 98.9 %all-to-all-start.1 = ((bf16[8,512,512]{2,1,0:T(8,128)(2,1)}), bf16[8,512,512]{2,1,0:T(8,128)(2,1)}, u32[]{:S(2)}, u32[]{:S(2)}) async-start(bf16[8,512,512]{2,1,0:T(8,128)(2,1)} %bitcast.188), calls=%async_computation.1 | async-start | bytes 8388608 | tf_op jit(solution)/shard_map/all_to_all | solution.py:94
  157.3 5.8 copy-start.19
  157.3 9.8 copy-start.25
  157.3 11.2 copy-start.17
  163.0 4.1 copy-start.9
  173.6 14.5 %copy-start.2 = (bf16[4096,2,256]{0,2,1:T(8,128)(2,1)}, bf16[4096,2,256]{0,2,1:T(8,128)(2,1)S(1)}, u32[]{:S(2)}) copy-start(bf16[4096,2,256]{0,2,1:T(8,128)(2,1)S(1)} %get-tuple-element.100) | copy-start | bytes 12582916
  188.2 3.8 copy-start.35
  196.6 187.0 %all-to-all-start.2 = ((f32[8,512,512]{2,1,0:T(8,128)}), f32[8,512,512]{2,1,0:T(8,128)}, u32[]{:S(2)}, u32[]{:S(2)}) async-start(f32[8,512,512]{2,1,0:T(8,128)} %fusion.65), calls=%async_computation.2 | async-start | bytes 16777216 | tf_op jit(solution)/shard_map/all_to_all | solution.py:83
  201.6 449.4 %all-reduce.10.cloned.1.call-start = ((), (), s32[]{:S(2)}) async-start(), calls=%async_computation.6 | async-start | bytes 16777216 | tf_op jit(solution)/shard_map/psum | solution.py:87
  396.4 76.3 %copy-start.50 = (f32[512]{0:T(512)S(1)}, f32[512]{0:T(512)}, u32[]{:S(2)}) copy-start(f32[512]{0:T(512)} %param.23) | copy-start | bytes 6148
  472.7 2.5 copy-start.15
  476.4 3.1 copy-start.27
  476.4 3.1 copy-start.53
  491.3 3.5 copy-start.24
  651.0 4.7 copy-start.5
  651.0 5.9 copy-start.21
  777.9 2.8 copy-start.3
  784.6 3.9 copy-start.10
  814.8 10.7 copy-start.20
  832.4 10.4 copy-start.18
  842.9 5.3 copy-start.31
  842.9 5.3 copy-start.37
  855.4 297.9 %all-to-all-start.4 = ((f32[8,512,512]{2,1,0:T(8,128)}), f32[8,512,512]{2,1,0:T(8,128)}, u32[]{:S(2)}, u32[]{:S(2)}) async-start(f32[8,512,512]{2,1,0:T(8,128)} %bitcast.194), calls=%async_computation.4 | async-start | bytes 16777216 | tf_op jit(solution)/shard_map/all_to_all | solution.py:83
  860.4 4.7 copy-start.23
  860.4 290.7 %all-reduce.8.cloned.1.call-start = ((), (), s32[]{:S(2)}) async-start(), calls=%async_computation.5 | async-start | bytes 6291456 | tf_op jit(solution)/shard_map/psum | solution.py:256
  860.4 4.6 copy-start.6
  865.1 2.5 copy-start.12
  865.1 2.7 copy-start.29
  1166.2 77.8 %copy-start.8 = (bf16[2048,512]{1,0:T(8,128)(2,1)S(1)}, bf16[2048,512]{1,0:T(8,128)(2,1)}, u32[]{:S(2)}) copy-start(bf16[2048,512]{1,0:T(8,128)(2,1)} %param.16) | copy-start | bytes 6291460
  1166.2 77.8 %copy-start.39 = (f32[2048]{0:T(1024)S(1)}, f32[2048]{0:T(1024)}, u32[]{:S(2)}) copy-start(f32[2048]{0:T(1024)} %copy-done.38) | copy-start | bytes 24580
  1166.2 77.8 %copy-start.49 = (f32[512]{0:T(512)S(1)}, f32[512]{0:T(512)}, u32[]{:S(2)}) copy-start(f32[512]{0:T(512)} %param.24) | copy-start | bytes 6148
  1166.2 81.2 %copy-start.46 = (f32[2048]{0:T(1024)S(1)}, f32[2048]{0:T(1024)}, u32[]{:S(2)}) copy-start(f32[2048]{0:T(1024)} %copy-done.45) | copy-start | bytes 24580
  1166.2 81.2 %copy-start.43 = (f32[2048]{0:T(1024)S(1)}, f32[2048]{0:T(1024)}, u32[]{:S(2)}) copy-start(f32[2048]{0:T(1024)} %copy-done.42) | copy-start | bytes 24580
  1244.0 7.1 copy-start.13
  1244.0 7.1 copy-start.14
  1244.0 7.1 copy-start.16
  1244.0 7.1 copy-start.51
  1244.0 7.1 copy-start.54
  1251.1 42.9 %copy-start.40 = (f32[128,512]{1,0:T(8,128)S(1)}, f32[128,512]{1,0:T(8,128)}, u32[]{:S(2)}) copy-start(f32[128,512]{1,0:T(8,128)} %get-tuple-element.113) | copy-start | bytes 786436
  1251.1 48.2 %copy-start.1 = (bf16[512,512]{1,0:T(8,128)(2,1)S(1)}, bf16[512,512]{1,0:T(8,128)(2,1)}, u32[]{:S(2)}) copy-start(bf16[512,512]{1,0:T(8,128)(2,1)} %param.30) | copy-start | bytes 1572868
  (13 other events, 19.1 us)
Sparse Core Ops, SparseCore 0:
  498.1 152.8 all-reduce.9
  874.5 276.5 all-reduce.7
where the time goes:
time: 1320 us; the launch traced here: 1310 us
  waiting for transfers between devices  704 us (53%)
  blocking collectives  288 us (22%)
  matrix products  143 us (11%)
  other arithmetic  66.3 us (5%)
  local copies, waits for them, and re-layouts  66.1 us (5%)
  starting transfers between devices  23.7 us (2%)
  between operations  15.4 us (1%)
    psum x1, waiting for transfers between devices, per_device(): lax.psum((grad_qkv_weight, grad_out_weight, grad_out_bias, grad_norm1_gai...  277 us
    all_to_all x2, waiting for transfers between devices, home_rows(): lax.all_to_all(partial_rows, 'dp', split_axis=0, concat_axis=0, tiled=True)  182 us
    psum x2, blocking collectives, home_rows(): return lax.psum(returned[slot_index], 'mp').astype(jnp.bfloat16)  154 us
    psum x1, waiting for transfers between devices, over_units(): return lax.psum(partial_rows, 'mp')  153 us
    all_to_all x1, blocking collectives, per_device(): lax.all_to_all(to_slots(grad_branch), 'dp', split_axis=0, concat_axis=0,...  98.9 us
    all_to_all x1, waiting for transfers between devices, per_device(): lax.all_to_all(to_slots(normed_low), 'dp', split_axis=0, concat_axis=0, t...  91.9 us
    psum x1, blocking collectives, per_device(): lax.psum((grad_qkv_weight, grad_out_weight, grad_out_bias, grad_norm1_gai...  35.4 us
    scatter x2, other arithmetic, to_slots(): jnp.zeros((slots,) + rows.shape[1:], rows.dtype).at[slot_index].set(rows)  26.9 us
  transfers between devices with their start and end apart: 6, of which 4 were waited for; matrix products, arithmetic and copies ran while one was open for 2% of the time, Pallas kernels for 0%

commit v1 on v0

--- a/solution.py
+++ b/solution.py
@@ -80,7 +80,19 @@
         return jnp.zeros((slots,) + rows.shape[1:], rows.dtype).at[slot_index].set(rows)
 
     def home_rows(partial_rows):
-        returned = lax.all_to_all(partial_rows, "dp", split_axis=0, concat_axis=0, tiled=True)
+        ways, here = (lax.axis_size("dp"), lax.axis_index("dp"))
+        width = partial_rows.shape[0] // ways
+        lengths = list(partial_rows.shape)
+        lengths[0] = width
+        height = lengths[0]
+        lengths[0] = height * ways
+        full = jnp.zeros(lengths, partial_rows.dtype)
+        for mask in range(ways):
+            part = lax.dynamic_slice_in_dim(partial_rows, (here ^ mask) * width, width, axis=0)
+            if mask:
+                part = lax.ppermute(part, "dp", [(d, d ^ mask) for d in range(ways)])
+            full = lax.dynamic_update_slice_in_dim(full, part, (here ^ mask) * height, axis=0)
+        returned = full
         return lax.psum(returned[slot_index], "mp").astype(jnp.bfloat16)
 
     def over_units(partial_rows):

time: 1320 us -> 1260 us (0.955)
  waiting for transfers between devices: 704 us -> 635 us
  local copies, waits for them, and re-layouts: 66.1 us -> 99.8 us
  blocking collectives: 288 us -> 258 us
  starting transfers between devices: 23.7 us -> 42.2 us
    psum x1, waiting for transfers between devices: 277 us -> 0.01 us  [per_device(): lax.psum((grad_qkv_weight, grad_out_weight, grad_out_bias, grad_norm1_gai...]
    ppermute x0 -> x14, waiting for transfers between devices: none -> 261 us  [home_rows(): part = lax.ppermute(part, 'dp', [(d, d ^ mask) for d in range(ways)])]
    all_to_all x1 -> x0, blocking collectives: 98.9 us -> none  [per_device(): lax.all_to_all(to_slots(grad_branch), 'dp', split_axis=0, concat_axis=0,...]
    all_to_all x2 -> x1, waiting for transfers between devices: 182 us -> 89.3 us  [per_device(): lax.all_to_all(to_slots(grad_branch), 'dp', split_axis=0, concat_axis=0,...]
    psum x1, blocking collectives: 35.4 us -> 104 us  [per_device(): lax.psum((grad_qkv_weight, grad_out_weight, grad_out_bias, grad_norm1_gai...]
    psum x1, waiting for transfers between devices: 153 us -> 193 us  [over_units(): return lax.psum(partial_rows, 'mp')]
    dynamic_update_slice x0 -> x14, local copies, waits for them, and re-layouts: none -> 23.5 us  [home_rows(): lax.dynamic_update_slice_in_dim(full, part, (here ^ mask) * height, axis=0)]
    ppermute x0 -> x14, starting transfers between devices: none -> 23 us  [home_rows(): part = lax.ppermute(part, 'dp', [(d, d ^ mask) for d in range(ways)])]
  transfers between devices with their start and end apart: 6 -> 19, of which waited for: 4 -> 11; matrix products, arithmetic and copies ran while one was open for 2% -> 7% of each run, Pallas kernels for 0% -> 0%
where the time goes in v1:
time: 1260 us; the launch traced here: 1250 us
  waiting for transfers between devices  635 us (50%)
  blocking collectives  258 us (20%)
  matrix products  138 us (11%)
  local copies, waits for them, and re-layouts  99.8 us (8%)
  other arithmetic  64.4 us (5%)
  starting transfers between devices  42.2 us (3%)
  between operations  15.6 us (1%)
    ppermute x14, waiting for transfers between devices, home_rows(): part = lax.ppermute(part, 'dp', [(d, d ^ mask) for d in range(ways)])  261 us
    psum x1, waiting for transfers between devices, over_units(): return lax.psum(partial_rows, 'mp')  193 us
    psum x2, blocking collectives, home_rows(): return lax.psum(returned[slot_index], 'mp').astype(jnp.bfloat16)  153 us
    psum x1, blocking collectives, per_device(): lax.psum((grad_qkv_weight, grad_out_weight, grad_out_bias, grad_norm1_gai...  104 us
    all_to_all x1, waiting for transfers between devices, per_device(): lax.all_to_all(to_slots(normed_low), 'dp', split_axis=0, concat_axis=0, t...  91.8 us
    all_to_all x1, waiting for transfers between devices, per_device(): lax.all_to_all(to_slots(grad_branch), 'dp', split_axis=0, concat_axis=0,...  89.3 us
    scatter x2, other arithmetic, to_slots(): jnp.zeros((slots,) + rows.shape[1:], rows.dtype).at[slot_index].set(rows)  27 us
    gather x2, local copies, waits for them, and re-layouts, home_rows(): return lax.psum(returned[slot_index], 'mp').astype(jnp.bfloat16)  25.8 us
  transfers between devices with their start and end apart: 19, of which 11 were waited for; matrix products, arithmetic and copies ran while one was open for 7% of the time, Pallas kernels for 0%

profile of v1, /device:TPU:0, one launch (start us, length us, event | category | flops | bytes accessed | tf_op | source)
XLA Modules:
  0.0 1252.0 jit_solution(16546400905667354888)
XLA Ops:
  13.1 14.6 %scatter_custom_fusion = bf16[4096]{0:T(1024)(128)(2,1)S(1)} fusion(s32[2048]{0:T(1024)S(1)} %bitcast.211, bf16[2048]{0:T(1024)(128)(2,1)S(1)} %add_convert_fusion.3, bf16[]{:T(256)} %constant.52.clone.1), kind=kCustom, calls=%fused_computation.208 | custom fusion | bytes 8194 | tf_op jit(solution)/shard_map/scatter | solution.py:80
  29.5 7.3 all-to-all-start
  40.4 13.3 %scatter_custom_fusion.1 = bf16[4096,512]{1,0:T(8,128)(2,1)} fusion(s32[2048]{0:T(1024)S(1)} %bitcast.212, bf16[2048,512]{1,0:T(8,128)(2,1)S(1)} %copy-done.9, f32[512]{0:T(512)S(1)} %copy-done.66, f32[512]{0:T(512)S(1)} %copy-done.62, f32[2048]{0:T(1024)S(1)} %fusion.96, f32[2048]{0:T(1024)S(1)} %broadcast_multiply_fusion.7, bf16[]{:T(256)} %constant.52.clone.1), kind=kCustom, calls=%fused_computation.90 | custom fusion | flops 6291456 | bytes 6311938 | tf_op jit(solution)/shard_map/scatter | solution.py:80
  53.7 6.1 all-to-all-start.1
  60.8 91.8 %all-to-all-done.1 = bf16[8,512,512]{2,1,0:T(8,128)(2,1)} async-done(((bf16[8,512,512]{2,1,0:T(8,128)(2,1)}), bf16[8,512,512]{2,1,0:T(8,128)(2,1)}, u32[]{:S(2)}, u32[]{:S(2)}) %all-to-all-start.1) | async-done | bytes 4194336 | tf_op jit(solution)/shard_map/all_to_all | solution.py:106
  152.6 4.0 fusion.116
  157.9 5.1 fusion.2
  165.7 5.1 fusion.3
  182.1 4.3 broadcast.186.clone
  196.0 16.5 %collective-permute-done = f32[512,512]{1,0:T(8,128)S(1)} collective-permute-done((f32[512,512]{1,0:T(8,128)S(1)}, f32[512,512]{1,0:T(8,128)S(1)}, u32[]{:S(2)}, u32[]{:S(2)}) %collective-permute-start) | collective-permute-done | bytes 1048608 | tf_op jit(solution)/shard_map/ppermute | solution.py:93
  212.5 3.5 collective-permute-start.5
  216.0 42.9 %collective-permute-done.1 = f32[512,512]{1,0:T(8,128)S(1)} collective-permute-done((f32[512,512]{1,0:T(8,128)S(1)}, f32[512,512]{1,0:T(8,128)S(1)}, u32[]{:S(2)}, u32[]{:S(2)}) %collective-permute-start.1) | collective-permute-done | bytes 1048608 | tf_op jit(solution)/shard_map/ppermute | solution.py:93
  262.1 16.8 %collective-permute-done.2 = f32[512,512]{1,0:T(8,128)S(1)} collective-permute-done((f32[512,512]{1,0:T(8,128)S(1)}, f32[512,512]{1,0:T(8,128)S(1)}, u32[]{:S(2)}, u32[]{:S(2)}) %collective-permute-start.2) | collective-permute-done | bytes 1048608 | tf_op jit(solution)/shard_map/ppermute | solution.py:93
  281.0 51.4 %collective-permute-done.4 = f32[512,512]{1,0:T(8,128)S(1)} collective-permute-done((f32[512,512]{1,0:T(8,128)S(1)}, f32[512,512]{1,0:T(8,128)S(1)}, u32[]{:S(2)}, u32[]{:S(2)}) %collective-permute-start.4) | collective-permute-done | bytes 1048608 | tf_op jit(solution)/shard_map/ppermute | solution.py:93
  335.7 12.9 %gather_fusion = f32[2048,512]{1,0:T(8,128)} fusion(f32[4096,512]{1,0:T(8,128)} %constant_dynamic-update-slice_fusion.6, s32[2048]{0:T(1024)S(1)} %broadcast_clamp_fusion), kind=kCustom, calls=%fused_computation | custom fusion | bytes 8396800 | tf_op jit(solution)/shard_map/gather | solution.py:96
  348.5 76.4 %all-reduce.11 = bf16[2048,512]{1,0:T(8,128)(2,1)} all-reduce(f32[2048,512]{1,0:T(8,128)} %gather_fusion), channel_id=1, replica_groups=mesh['dp'=8,'mp'=4] {'mp'}, use_global_device_ids=true, to_apply=%region_10.11 | all-reduce | flops 1048576 | bytes 6291456 | tf_op jit(solution)/shard_map/psum | solution.py:96
  431.8 10.6 convert_reduce_fusion.3
  450.0 192.9 %all-reduce.10.cloned.1.call-done = (f32[2048,512]{1,0:T(8,128)}, f32[2048,512]{1,0:T(8,128)}) async-done(((f32[2048,512]{1,0:T(8,128)}, f32[2048,512]{1,0:T(8,128)}), (f32[2048,512]{1,0:T(8,128)}, f32[2048,512]{1,0:T(8,128)})) %all-reduce.10.cloned.1.call-update) | async-done | bytes 8388624 | tf_op jit(solution)/shard_map/psum | solution.py:99
  642.9 4.4 multiply_reduce_fusion
  651.5 13.7 %scatter_custom_fusion.2 = bf16[4096,512]{1,0:T(8,128)(2,1)} fusion(s32[2048]{0:T(1024)S(1)} %bitcast.214, bf16[]{:T(256)} %constant.52.clone.1, bf16[2048,512]{1,0:T(8,128)(2,1)} %param.17, f32[2048,512]{1,0:T(8,128)} %get-tuple-element.82, f32[2048]{0:T(1024)S(1)} %negate_multiply_fusion.2), kind=kCustom, calls=%fused_computation.92 | custom fusion | flops 4194304 | bytes 10493954 | tf_op jit(solution)/shard_map/scatter | solution.py:80
  665.2 5.5 all-to-all-start.2
  670.8 3.8 fusion.122
  674.6 89.3 %all-to-all-done.2 = bf16[8,512,512]{2,1,0:T(8,128)(2,1)} async-done(((bf16[8,512,512]{2,1,0:T(8,128)(2,1)}), bf16[8,512,512]{2,1,0:T(8,128)(2,1)}, u32[]{:S(2)}, u32[]{:S(2)}) %all-to-all-start.2) | async-done | bytes 4194336 | tf_op jit(solution)/shard_map/all_to_all | solution.py:191
  763.9 4.4 convolution_convert_fusion
  770.2 6.2 fusion.54
  776.4 3.9 fusion.51
  782.7 5.6 fusion.120
  788.8 5.9 fusion.56
  800.3 5.7 fusion.80
  809.3 10.3 fusion.114
  819.7 4.7 fusion.15
  826.7 10.4 fusion.115
  837.2 3.7 fusion.14
  842.5 7.1 convolution_bitcast_fusion
  850.7 5.9 constant_dynamic-slice_fusion.13
  866.5 5.0 convolution_bitcast_fusion.1
  871.4 9.1 collective-permute-done.7
  880.5 3.5 collective-permute-start.12
  884.0 41.1 %collective-permute-done.8 = f32[512,512]{1,0:T(8,128)S(1)} collective-permute-done((f32[512,512]{1,0:T(8,128)S(1)}, f32[512,512]{1,0:T(8,128)S(1)}, u32[]{:S(2)}, u32[]{:S(2)}) %collective-permute-start.8) | collective-permute-done | bytes 1048608 | tf_op jit(solution)/shard_map/ppermute | solution.py:93
  926.1 3.6 fusion.121
  934.3 23.1 %collective-permute-done.9 = f32[512,512]{1,0:T(8,128)} collective-permute-done((f32[512,512]{1,0:T(8,128)}, f32[512,512]{1,0:T(8,128)}, u32[]{:S(2)}, u32[]{:S(2)}) %collective-permute-start.9) | collective-permute-done | bytes 1048608 | tf_op jit(solution)/shard_map/ppermute | solution.py:93
  961.9 59.7 %collective-permute-done.11 = f32[512,512]{1,0:T(8,128)} collective-permute-done((f32[512,512]{1,0:T(8,128)}, f32[512,512]{1,0:T(8,128)}, u32[]{:S(2)}, u32[]{:S(2)}) %collective-permute-start.11) | collective-permute-done | bytes 1048608 | tf_op jit(solution)/shard_map/ppermute | solution.py:93
  1028.6 13.0 %gather_fusion.1 = f32[2048,512]{1,0:T(8,128)} fusion(f32[4096,512]{1,0:T(8,128)} %constant_dynamic-update-slice_fusion.13, s32[2048]{0:T(1024)S(1)} %copy-done.54), kind=kCustom, calls=%fused_computation.1 | custom fusion | bytes 8396800 | tf_op jit(solution)/shard_map/gather | solution.py:96
  1041.6 76.7 %all-reduce.12 = bf16[2048,512]{1,0:T(8,128)(2,1)} all-reduce(f32[2048,512]{1,0:T(8,128)} %gather_fusion.1), channel_id=1, replica_groups=mesh['dp'=8,'mp'=4] {'mp'}, use_global_device_ids=true, to_apply=%region_21.22 | all-reduce | flops 1048576 | bytes 6291456 | tf_op jit(solution)/shard_map/psum | solution.py:96
  1118.3 3.4 convert_reduce_fusion
  1121.8 3.6 fusion.24
  1125.4 7.5 convert_reduce_fusion.2
  1132.9 104.4 %all-reduce = (f32[512]{0:T(512)}, f32[512]{0:T(512)}, f32[512]{0:T(512)}, f32[512]{0:T(512)}, f32[512]{0:T(512)}, /*index=5*/f32[512]{0:T(512)}, f32[512]{0:T(512)}) all-reduce(f32[512]{0:T(512)S(1)} %get-tuple-element.58, f32[512]{0:T(512)S(1)} %get-tuple-element.54, ...), channel_id=1, replica_groups=mesh['dp'=8,'mp'=4] {'dp'}, use_global_device_ids=true, to_apply=%region_27.28 | all-reduce | flops 3584 | bytes 28672 | tf_op jit(solution)/shard_map/psum | solution.py:268
  (255 shorter events, 116.8 us)
Async XLA Ops:
  7.2 423.6 %copy-start = (bf16[512,512]{1,0:T(8,128)(2,1)S(1)}, bf16[512,512]{1,0:T(8,128)(2,1)}, u32[]{:S(2)}) copy-start(bf16[512,512]{1,0:T(8,128)(2,1)} %param.30) | copy-start | bytes 1572868
  7.2 31.5 %copy-start.9 = (bf16[2048,512]{1,0:T(8,128)(2,1)S(1)}, bf16[2048,512]{1,0:T(8,128)(2,1)}, u32[]{:S(2)}) copy-start(bf16[2048,512]{1,0:T(8,128)(2,1)} %param.16) | copy-start | bytes 6291460
  7.2 33.2 %copy-start.66 = (f32[512]{0:T(512)S(1)}, f32[512]{0:T(512)}, u32[]{:S(2)}) copy-start(f32[512]{0:T(512)} %param.25) | copy-start | bytes 6148
  7.2 33.2 %copy-start.62 = (f32[512]{0:T(512)S(1)}, f32[512]{0:T(512)}, u32[]{:S(2)}) copy-start(f32[512]{0:T(512)} %param.24) | copy-start | bytes 6148
  29.5 24.2 %all-to-all-start = ((bf16[8,2,256]{2,1,0:T(2,128)(2,1)}), bf16[8,2,256]{2,1,0:T(2,128)(2,1)S(1)}, u32[]{:S(2)}, u32[]{:S(2)}) async-start(bf16[8,2,256]{2,1,0:T(2,128)(2,1)} %reshape.242), calls=%async_computation | async-start | bytes 16384 | tf_op jit(solution)/shard_map/all_to_all | solution.py:107
  38.7 15.0 %copy-start.46 = (f32[2048]{0:T(1024)}, f32[2048]{0:T(1024)S(1)}, u32[]{:S(2)}) copy-start(f32[2048]{0:T(1024)S(1)} %broadcast_multiply_fusion.7) | copy-start | bytes 24580
  40.4 13.3 %copy-start.50 = (f32[2048]{0:T(1024)}, f32[2048]{0:T(1024)S(1)}, u32[]{:S(2)}) copy-start(f32[2048]{0:T(1024)S(1)} %fusion.96) | copy-start | bytes 24580
  53.7 98.9 %all-to-all-start.1 = ((bf16[8,512,512]{2,1,0:T(8,128)(2,1)}), bf16[8,512,512]{2,1,0:T(8,128)(2,1)}, u32[]{:S(2)}, u32[]{:S(2)}) async-start(bf16[8,512,512]{2,1,0:T(8,128)(2,1)} %bitcast.174), calls=%async_computation.1 | async-start | bytes 8388608 | tf_op jit(solution)/shard_map/all_to_all | solution.py:106
  59.8 583.0 %all-reduce.10.cloned.1.call-start = ((), (), s32[]{:S(2)}) async-start(), calls=%async_computation.4 | async-start | bytes 16777216 | tf_op jit(solution)/shard_map/psum | solution.py:99
  157.3 8.5 copy-start.17
  157.3 18.8 %copy-start.24 = (bf16[4096,1,128]{0,2,1:T(8,128)(2,1)}, bf16[4096,1,128]{0,2,1:T(8,128)(2,1)S(1)}, u32[]{:S(2)}) copy-start(bf16[4096,1,128]{0,2,1:T(8,128)(2,1)S(1)} %get-tuple-element.103) | copy-start | bytes 3145732
  163.0 13.1 %copy-start.11 = (bf16[4096,2,256]{0,2,1:T(8,128)(2,1)}, bf16[4096,2,256]{0,2,1:T(8,128)(2,1)S(1)}, u32[]{:S(2)}) copy-start(bf16[4096,2,256]{0,2,1:T(8,128)(2,1)S(1)} %get-tuple-element.114) | copy-start | bytes 12582916
  188.7 23.8 %collective-permute-start = (f32[512,512]{1,0:T(8,128)S(1)}, f32[512,512]{1,0:T(8,128)S(1)}, u32[]{:S(2)}, u32[]{:S(2)}) collective-permute-start(f32[512,512]{1,0:T(8,128)S(1)} %get-tuple-element.99), channel_id=1, source_target_pairs={{0,4},{4,0},{8,12},{12,8},{16,20},{20,16},{24,28},{28,24},{1,5},{5... | collective-permute-start | bytes 3145736 | tf_op jit(solution)/shard_map/ppermute | solution.py:93
  190.1 68.8 %collective-permute-start.1 = (f32[512,512]{1,0:T(8,128)S(1)}, f32[512,512]{1,0:T(8,128)S(1)}, u32[]{:S(2)}, u32[]{:S(2)}) collective-permute-start(f32[512,512]{1,0:T(8,128)S(1)} %get-tuple-element.98), channel_id=1, source_target_pairs={{0,8},{4,12},{8,0},{12,4},{16,24},{20,28},{24,16},{28,20},{1,9},{5... | collective-permute-start | bytes 3145736 | tf_op jit(solution)/shard_map/ppermute | solution.py:93
  190.1 88.7 %collective-permute-start.2 = (f32[512,512]{1,0:T(8,128)S(1)}, f32[512,512]{1,0:T(8,128)S(1)}, u32[]{:S(2)}, u32[]{:S(2)}) collective-permute-start(f32[512,512]{1,0:T(8,128)S(1)} %get-tuple-element.97), channel_id=1, source_target_pairs={{0,12},{4,8},{8,4},{12,0},{16,28},{20,24},{24,20},{28,16},{1,13},{... | collective-permute-start | bytes 3145736 | tf_op jit(solution)/shard_map/ppermute | solution.py:93
  192.1 87.8 %collective-permute-start.3 = (f32[512,512]{1,0:T(8,128)S(1)}, f32[512,512]{1,0:T(8,128)S(1)}, u32[]{:S(2)}, u32[]{:S(2)}) collective-permute-start(f32[512,512]{1,0:T(8,128)S(1)} %get-tuple-element.96), channel_id=1, source_target_pairs={{0,16},{4,20},{8,24},{12,28},{16,0},{20,4},{24,8},{28,12},{1,17},{... | collective-permute-start | bytes 3145736 | tf_op jit(solution)/shard_map/ppermute | solution.py:93
  193.0 139.4 %collective-permute-start.4 = (f32[512,512]{1,0:T(8,128)S(1)}, f32[512,512]{1,0:T(8,128)S(1)}, u32[]{:S(2)}, u32[]{:S(2)}) collective-permute-start(f32[512,512]{1,0:T(8,128)S(1)} %get-tuple-element.95), channel_id=1, source_target_pairs={{0,20},{4,16},{8,28},{12,24},{16,4},{20,0},{24,12},{28,8},{1,21},{... | collective-permute-start | bytes 3145736 | tf_op jit(solution)/shard_map/ppermute | solution.py:93
  212.5 121.0 %collective-permute-start.5 = (f32[512,512]{1,0:T(8,128)S(1)}, f32[512,512]{1,0:T(8,128)S(1)}, u32[]{:S(2)}, u32[]{:S(2)}) collective-permute-start(f32[512,512]{1,0:T(8,128)S(1)} %get-tuple-element.94), channel_id=1, source_target_pairs={{0,24},{4,28},{8,16},{12,20},{16,8},{20,12},{24,0},{28,4},{1,25},{... | collective-permute-start | bytes 3145736 | tf_op jit(solution)/shard_map/ppermute | solution.py:93
  259.0 75.6 %collective-permute-start.6 = (f32[512,512]{1,0:T(8,128)S(1)}, f32[512,512]{1,0:T(8,128)S(1)}, u32[]{:S(2)}, u32[]{:S(2)}) collective-permute-start(f32[512,512]{1,0:T(8,128)S(1)} %get-tuple-element.93), channel_id=1, source_target_pairs={{0,28},{4,24},{8,20},{12,16},{16,12},{20,8},{24,4},{28,0},{1,29},{... | collective-permute-start | bytes 3145736 | tf_op jit(solution)/shard_map/ppermute | solution.py:93
  260.0 75.7 %copy-start.53 = (s32[2048]{0:T(1024)}, s32[2048]{0:T(1024)S(1)}, u32[]{:S(2)}) copy-start(s32[2048]{0:T(1024)S(1)} %broadcast_clamp_fusion) | copy-start | bytes 24580
  348.5 76.4 %copy-start.64 = (f32[512]{0:T(512)S(1)}, f32[512]{0:T(512)}, u32[]{:S(2)}) copy-start(f32[512]{0:T(512)} %param.23) | copy-start | bytes 6148
  665.2 98.7 %all-to-all-start.2 = ((bf16[8,512,512]{2,1,0:T(8,128)(2,1)}), bf16[8,512,512]{2,1,0:T(8,128)(2,1)}, u32[]{:S(2)}, u32[]{:S(2)}) async-start(bf16[8,512,512]{2,1,0:T(8,128)(2,1)} %bitcast.175), calls=%async_computation.2 | async-start | bytes 8388608 | tf_op jit(solution)/shard_map/all_to_all | solution.py:191
  670.7 566.7 %all-reduce.8.cloned.1.call-start = ((), (), s32[]{:S(2)}) async-start(), calls=%async_computation.3 | async-start | bytes 6291456 | tf_op jit(solution)/shard_map/psum | solution.py:268
  800.3 9.0 copy-start.26
  800.3 9.0 copy-start.42
  809.3 10.3 copy-start.20
  809.3 10.3 copy-start.49
  826.7 10.5 copy-start.18
  856.6 14.8 %copy-start.2 = (f32[4096,512]{1,0:T(8,128)}, f32[4096,512]{1,0:T(8,128)S(1)}, u32[]{:S(2)}) copy-start(f32[4096,512]{1,0:T(8,128)S(1)} %get-tuple-element.92) | copy-start | bytes 25165828
  856.6 9.9 copy-start.36
  856.6 9.9 copy-start.37
  856.6 9.9 copy-start.38
  856.6 23.9 %collective-permute-start.7 = (f32[512,512]{1,0:T(8,128)S(1)}, f32[512,512]{1,0:T(8,128)S(1)}, u32[]{:S(2)}, u32[]{:S(2)}) collective-permute-start(f32[512,512]{1,0:T(8,128)S(1)} %get-tuple-element.91), channel_id=1, source_target_pairs={{0,4},{4,0},{8,12},{12,8},{16,20},{20,16},{24,28},{28,24},{1,5},{5... | collective-permute-start | bytes 3145736 | tf_op jit(solution)/shard_map/ppermute | solution.py:93
  858.1 67.0 %collective-permute-start.8 = (f32[512,512]{1,0:T(8,128)S(1)}, f32[512,512]{1,0:T(8,128)S(1)}, u32[]{:S(2)}, u32[]{:S(2)}) collective-permute-start(f32[512,512]{1,0:T(8,128)S(1)} %get-tuple-element.90), channel_id=1, source_target_pairs={{0,8},{4,12},{8,0},{12,4},{16,24},{20,28},{24,16},{28,20},{1,9},{5... | collective-permute-start | bytes 3145736 | tf_op jit(solution)/shard_map/ppermute | solution.py:93
  860.6 96.8 %collective-permute-start.9 = (f32[512,512]{1,0:T(8,128)}, f32[512,512]{1,0:T(8,128)}, u32[]{:S(2)}, u32[]{:S(2)}) collective-permute-start(f32[512,512]{1,0:T(8,128)} %get-tuple-element.89), channel_id=1, source_target_pairs={{0,12},{4,8},{8,4},{12,0},{16,28},{20,24},{24,20},{28,16},{1,13},{... | collective-permute-start | bytes 3145736 | tf_op jit(solution)/shard_map/ppermute | solution.py:93
  862.6 97.0 %collective-permute-start.10 = (f32[512,512]{1,0:T(8,128)}, f32[512,512]{1,0:T(8,128)}, u32[]{:S(2)}, u32[]{:S(2)}) collective-permute-start(f32[512,512]{1,0:T(8,128)} %get-tuple-element.88), channel_id=1, source_target_pairs={{0,16},{4,20},{8,24},{12,28},{16,0},{20,4},{24,8},{28,12},{1,17},{... | collective-permute-start | bytes 3145736 | tf_op jit(solution)/shard_map/ppermute | solution.py:93
  863.4 158.2 %collective-permute-start.11 = (f32[512,512]{1,0:T(8,128)}, f32[512,512]{1,0:T(8,128)}, u32[]{:S(2)}, u32[]{:S(2)}) collective-permute-start(f32[512,512]{1,0:T(8,128)} %get-tuple-element.87), channel_id=1, source_target_pairs={{0,20},{4,16},{8,28},{12,24},{16,4},{20,0},{24,12},{28,8},{1,21},{... | collective-permute-start | bytes 3145736 | tf_op jit(solution)/shard_map/ppermute | solution.py:93
  866.5 59.6 %copy-start.29 = (bf16[4096,2,64]{0,2,1:T(8,128)(2,1)S(1)}, bf16[4096,2,64]{0,2,1:T(8,128)(2,1)}, u32[]{:S(2)}) copy-start(bf16[4096,2,64]{0,2,1:T(8,128)(2,1)} %copy-done.28) | copy-start | bytes 3145732
  880.5 44.8 %copy-start.32 = (f32[512,512]{1,0:T(8,128)}, f32[512,512]{1,0:T(8,128)S(1)}, u32[]{:S(2)}) copy-start(f32[512,512]{1,0:T(8,128)S(1)} %collective-permute-done.7) | copy-start | bytes 3145732
  880.5 143.4 %collective-permute-start.12 = (f32[512,512]{1,0:T(8,128)S(1)}, f32[512,512]{1,0:T(8,128)}, u32[]{:S(2)}, u32[]{:S(2)}) collective-permute-start(f32[512,512]{1,0:T(8,128)S(1)} %get-tuple-element.86), channel_id=1, source_target_pairs={{0,24},{4,28},{8,16},{12,20},{16,8},{20,12},{24,0},{28,4},{1,25},{... | collective-permute-start | bytes 3145736 | tf_op jit(solution)/shard_map/ppermute | solution.py:93
  925.1 101.1 %collective-permute-start.13 = (f32[512,512]{1,0:T(8,128)S(1)}, f32[512,512]{1,0:T(8,128)}, u32[]{:S(2)}, u32[]{:S(2)}) collective-permute-start(f32[512,512]{1,0:T(8,128)S(1)} %get-tuple-element.85), channel_id=1, source_target_pairs={{0,28},{4,24},{8,20},{12,16},{16,12},{20,8},{24,4},{28,0},{1,29},{... | collective-permute-start | bytes 3145736 | tf_op jit(solution)/shard_map/ppermute | solution.py:93
  959.7 68.9 %copy-start.54 = (s32[2048]{0:T(1024)S(1)}, s32[2048]{0:T(1024)}, u32[]{:S(2)}) copy-start(s32[2048]{0:T(1024)} %copy-done.53) | copy-start | bytes 24580
  1041.5 76.7 %copy-start.10 = (bf16[2048,512]{1,0:T(8,128)(2,1)S(1)}, bf16[2048,512]{1,0:T(8,128)(2,1)}, u32[]{:S(2)}) copy-start(bf16[2048,512]{1,0:T(8,128)(2,1)} %param.16) | copy-start | bytes 6291460
  1041.5 76.7 %copy-start.47 = (f32[2048]{0:T(1024)S(1)}, f32[2048]{0:T(1024)}, u32[]{:S(2)}) copy-start(f32[2048]{0:T(1024)} %copy-done.46) | copy-start | bytes 24580
  1041.5 76.7 %copy-start.63 = (f32[512]{0:T(512)S(1)}, f32[512]{0:T(512)}, u32[]{:S(2)}) copy-start(f32[512]{0:T(512)} %param.24) | copy-start | bytes 6148
  1041.5 80.2 %copy-start.56 = (f32[2048]{0:T(1024)S(1)}, f32[2048]{0:T(1024)}, u32[]{:S(2)}) copy-start(f32[2048]{0:T(1024)} %copy-done.55) | copy-start | bytes 24580
  1041.5 80.2 %copy-start.51 = (f32[2048]{0:T(1024)S(1)}, f32[2048]{0:T(1024)}, u32[]{:S(2)}) copy-start(f32[2048]{0:T(1024)} %copy-done.50) | copy-start | bytes 24580
  1125.4 119.2 %copy-start.1 = (bf16[512,512]{1,0:T(8,128)(2,1)S(1)}, bf16[512,512]{1,0:T(8,128)(2,1)}, u32[]{:S(2)}) copy-start(bf16[512,512]{1,0:T(8,128)(2,1)} %param.30) | copy-start | bytes 1572868
  (40 other events, 183.6 us)
Sparse Core Ops, SparseCore 0:
  450.1 192.7 all-reduce.9
  929.8 207.9 all-reduce.7
